TPU v7x, 32 devices: a whole 2x2x4 slice. The times are simulated.
32 devices in a mesh: wide: 8 (over z, x), narrow: 4 (over y, core).
Axes of the slice: x: 2, y: 2, z: 4, core: 2. Of those that a mesh axis runs over, the one named last changes fastest.
Arguments:
- samples: bfloat16 [16384, 1024], P(('wide', 'narrow')), may hold values from -16 to 16
- centroid_table: bfloat16 [16384, 1024], P('wide', 'narrow'), may hold values from -6 to 6
- owner: int32 [16384], replicated, may hold values from 0 to 7, as said below
- slot: int32 [16384], replicated, may hold values from 0 to 2047, as said below
- assign: int32 [16384], P('wide'), may hold values from 0 to 16383, as said below
- codebook: float32 [8, 2048, 128], P('narrow'), may hold values from -16 to 16
Outputs:
- residual: bfloat16 [16384, 1024], P('wide', 'narrow')
- refined: float32 [8, 2048, 128], P('narrow')
Inputs may be any that keep to these rules, and one draw needn't show every extreme that they name: owner and slot give each coarse centroid a distinct storage position owner * 2048 + slot. `slot`: see owner. `assign`: in each aligned block of 2048 rows (the rows of one index of wide), at most 512 rows have centroids with one owner, and some owner has exactly 512.
All inputs are finite; a program needn't handle non-finite values.
Results may differ from a plain program's by a relative error of at most 0.0079.
Values may be sent and summed in bfloat16 or wider, within the bound.
No kernel may reach another device: no remote copies, remote signals or barrier semaphores. Data moves between devices by JAX's collectives and lax.ppermute only.
A program may use at most 64 MiB of HBM per device.

v0:
```python
import jax
import jax.numpy as jnp
from jax import lax
from jax.sharding import PartitionSpec as P

ITERS = 2
softness_level = 16.0
prior_weight = 1.0


def score_pass(blocks, narrow_words, codeword_norm_values):
    spaces = narrow_words.shape[0]
    words_count = narrow_words.shape[1]
    sub_width = narrow_words.shape[2]

    def block_step(running, row_block):
        inner_product_rows = jnp.einsum(
            "bms,mks->mbk", row_block, narrow_words, preferred_element_type=jnp.float32
        )
        score_matrix = (
            2.0 * inner_product_rows - codeword_norm_values[:, None, :]
        ) / softness_level
        weights_soft = jax.nn.softmax(score_matrix, axis=2).astype(jnp.bfloat16)
        totals = running[0] + jnp.einsum(
            "mbk,bms->mks", weights_soft, row_block, preferred_element_type=jnp.float32
        )
        return ((totals, running[1] + jnp.sum(weights_soft, axis=1, dtype=jnp.float32)), None)

    start = (
        jnp.zeros((spaces, words_count, sub_width), jnp.float32),
        jnp.zeros((spaces, words_count), jnp.float32),
    )
    (totals, counts), ignored = lax.scan(block_step, start, blocks)
    return (totals, counts)


def on_device(samples, centroid_table, owner, slot, assign, codebook):
    regrouped = lax.all_to_all(samples, "narrow", split_axis=1, concat_axis=0, tiled=True)
    group_rows = regrouped.shape[0]
    owner_of = owner[assign]
    slot_of = slot[assign]
    whole = lax.all_gather(centroid_table, "wide", axis=0, tiled=True)
    centre = jnp.take(whole, owner_of * centroid_table.shape[0] + slot_of, axis=0)
    residual = (regrouped.astype(jnp.float32) - centre.astype(jnp.float32)).astype(jnp.bfloat16)
    spaces = codebook.shape[0]
    sub_width = codebook.shape[2]
    block_size = 512
    blocks = residual.reshape(group_rows // block_size, block_size, spaces, sub_width)
    codewords = codebook
    narrow_words = codebook.astype(jnp.bfloat16)
    codeword_norm_values = jnp.sum(codebook * codebook, axis=2)
    for iteration in range(ITERS):
        narrow_words = codewords.astype(jnp.bfloat16)
        codeword_norm_values = jnp.sum(codewords * codewords, axis=2)
        totals, counts = score_pass(blocks, narrow_words, codeword_norm_values)
        totals, counts = lax.psum((totals, counts), "wide")
        codewords = (totals + prior_weight * codewords) / (counts[:, :, None] + prior_weight)
    return (residual, codewords)


def solution(mesh):
    return jax.shard_map(
        on_device,
        mesh=mesh,
        in_specs=(
            P(("wide", "narrow"), None),
            P("wide", "narrow"),
            P(),
            P(),
            P("wide"),
            P("narrow", None, None),
        ),
        out_specs=(P("wide", "narrow"), P("narrow", None, None)),
        check_vma=False,
    )
```

profile of v0, /device:TPU:0, one launch (start us, length us, event | category | flops | bytes accessed | tf_op | source)
XLA Modules:
  0.0 518.3 jit_solution(10853874548214603583)
XLA Ops:
  7.2 0.0 copy-start
  7.2 0.0 all-gather.2.cloned.1.call-start
  7.2 0.7 all-gather.2.cloned.1.call-update
  7.9 2.3 copy.14
  10.2 4.3 all-to-all-start
  14.5 0.0 copy-done.9
  14.5 0.0 copy-done
  14.5 0.0 copy-start.2
  14.5 11.8 %gather_fusion.1 = s32[2048]{0:T(1024)S(1)} fusion(s32[16384]{0:T(1024)S(1)} %copy-done, s32[2048]{0:T(1024)S(1)} %fusion.55), kind=kCustom, calls=%fused_computation.1 | custom fusion | bytes 24576 | tf_op jit(solution)/shard_map/gather | solution.py:41
  26.3 11.8 %gather_fusion = s32[2048]{0:T(1024)S(1)} fusion(s32[16384]{0:T(1024)S(1)} %copy-done.2, s32[2048]{0:T(1024)S(1)} %fusion.55), kind=kCustom, calls=%fused_computation | custom fusion | bytes 24576 | tf_op jit(solution)/shard_map/gather | solution.py:40
  38.2 3.9 multiply_reduce_fusion.1
  42.1 0.0 all-to-all-done
  42.1 2.6 fusion.66
  44.7 92.6 %all-gather.2.cloned.1.call-done = bf16[16384,256]{1,0:T(8,128)(2,1)} async-done(((bf16[2048,256]{1,0:T(8,128)(2,1)}), bf16[16384,256]{1,0:T(8,128)(2,1)}) %all-gather.2.cloned.1.call-update) | async-done | bytes 8388624 | tf_op jit(solution)/shard_map/all_gather | solution.py:42
  137.4 11.1 %gather_fusion.2 = bf16[2048,256]{1,0:T(8,128)(2,1)S(1)} fusion(bf16[16384,256]{1,0:T(8,128)(2,1)} %all-gather.2.cloned.1.call-done, s32[2048]{0:T(1024)S(1)} %broadcast_clamp_fusion), kind=kCustom, calls=%fused_computation.2 | custom fusion | bytes 2105344 | tf_op jit(solution)/shard_map/jit(_take)/gather | solution.py:43
  148.5 0.0 copy-start.7
  148.5 1.4 gather.15
  149.8 3.7 copy.16
  153.5 3.3 subtract_convert_fusion
  156.8 1.6 copy.18
  158.4 69.5 %while.26 = (s32[]{:T(128)}, f32[2,2048,128]{2,1,0:T(8,128)S(1)}, f32[2,2048]{1,0:T(2,128)S(1)}, bf16[4,512,2,128]{3,1,2,0:T(8,128)(2,1)S(1)}, bf16[2,2048,128]{...) while((s32[]{:T(128)}, f32[2,2048,128]{2,1,0:T(8,128)S(1)}, ...), condition=%wide.region_5.6_spmd.clone, body=%wide.region_1.5_spmd.clone.sunk | while | flops 1093670912 | bytes 31023212 | solution.py:33
  158.4 7.2 %fusion.87 = (f32[2,512]{1,0:T(2,128)S(1)}, f32[2,512,2048]{2,1,0:T(8,128)}) fusion(f32[2,2048]{1,0:T(2,128)S(1)} %get-tuple-element.277, bf16[2,2048,128]{2,1,0:T(8,128)(2,1)} %get-tuple-element.276, bf16[4,512,2,128]{3,1,2,0:T(8,128)(2,1)S(1)} %get-tuple-element.275, s32[]{:T(128)S(6)} %copy.24), kind=kOutput, calls=%fused_computation.70.clone.1 | convolution fusion | flops 547358720 | bytes 9719812 | tf_op jit(solution)/shard_map/while/body/eval_jaxpr/sub | solution.py:23
  165.6 5.5 %convert_reduce_fusion.4 = (f32[2,2048]{1,0:T(2,128)S(1)}, bf16[2,512,2048]{2,1,0:T(8,128)(2,1)}) fusion(f32[2,512,2048]{2,1,0:T(8,128)} %get-tuple-element.242, f32[2,512]{1,0:T(2,128)S(1)} %get-tuple-element.243), kind=kLoop, calls=%fused_computation.4.clone.1 | loop fusion | flops 8384512 | bytes 12603392 | tf_op jit(solution)/shard_map/while/body/eval_jaxpr/reduce_sum | solution.py:27
  171.1 4.7 convolution_add_fusion.4
  175.8 7.2 %fusion.87 = (f32[2,512]{1,0:T(2,128)S(1)}, f32[2,512,2048]{2,1,0:T(8,128)}) fusion(f32[2,2048]{1,0:T(2,128)S(1)} %get-tuple-element.277, bf16[2,2048,128]{2,1,0:T(8,128)(2,1)} %get-tuple-element.276, bf16[4,512,2,128]{3,1,2,0:T(8,128)(2,1)S(1)} %get-tuple-element.275, s32[]{:T(128)S(6)} %copy.24), kind=kOutput, calls=%fused_computation.70.clone.1 | convolution fusion | flops 547358720 | bytes 9719812 | tf_op jit(solution)/shard_map/while/body/eval_jaxpr/sub | solution.py:23
  183.0 5.5 %convert_reduce_fusion.4 = (f32[2,2048]{1,0:T(2,128)S(1)}, bf16[2,512,2048]{2,1,0:T(8,128)(2,1)}) fusion(f32[2,512,2048]{2,1,0:T(8,128)} %get-tuple-element.242, f32[2,512]{1,0:T(2,128)S(1)} %get-tuple-element.243), kind=kLoop, calls=%fused_computation.4.clone.1 | loop fusion | flops 8384512 | bytes 12603392 | tf_op jit(solution)/shard_map/while/body/eval_jaxpr/reduce_sum | solution.py:27
  188.5 4.7 convolution_add_fusion.4
  193.2 7.2 %fusion.87 = (f32[2,512]{1,0:T(2,128)S(1)}, f32[2,512,2048]{2,1,0:T(8,128)}) fusion(f32[2,2048]{1,0:T(2,128)S(1)} %get-tuple-element.277, bf16[2,2048,128]{2,1,0:T(8,128)(2,1)} %get-tuple-element.276, bf16[4,512,2,128]{3,1,2,0:T(8,128)(2,1)S(1)} %get-tuple-element.275, s32[]{:T(128)S(6)} %copy.24), kind=kOutput, calls=%fused_computation.70.clone.1 | convolution fusion | flops 547358720 | bytes 9719812 | tf_op jit(solution)/shard_map/while/body/eval_jaxpr/sub | solution.py:23
  200.3 5.5 %convert_reduce_fusion.4 = (f32[2,2048]{1,0:T(2,128)S(1)}, bf16[2,512,2048]{2,1,0:T(8,128)(2,1)}) fusion(f32[2,512,2048]{2,1,0:T(8,128)} %get-tuple-element.242, f32[2,512]{1,0:T(2,128)S(1)} %get-tuple-element.243), kind=kLoop, calls=%fused_computation.4.clone.1 | loop fusion | flops 8384512 | bytes 12603392 | tf_op jit(solution)/shard_map/while/body/eval_jaxpr/reduce_sum | solution.py:27
  205.9 4.7 convolution_add_fusion.4
  210.6 7.2 %fusion.87 = (f32[2,512]{1,0:T(2,128)S(1)}, f32[2,512,2048]{2,1,0:T(8,128)}) fusion(f32[2,2048]{1,0:T(2,128)S(1)} %get-tuple-element.277, bf16[2,2048,128]{2,1,0:T(8,128)(2,1)} %get-tuple-element.276, bf16[4,512,2,128]{3,1,2,0:T(8,128)(2,1)S(1)} %get-tuple-element.275, s32[]{:T(128)S(6)} %copy.24), kind=kOutput, calls=%fused_computation.70.clone.1 | convolution fusion | flops 547358720 | bytes 9719812 | tf_op jit(solution)/shard_map/while/body/eval_jaxpr/sub | solution.py:23
  217.7 5.5 %convert_reduce_fusion.4 = (f32[2,2048]{1,0:T(2,128)S(1)}, bf16[2,512,2048]{2,1,0:T(8,128)(2,1)}) fusion(f32[2,512,2048]{2,1,0:T(8,128)} %get-tuple-element.242, f32[2,512]{1,0:T(2,128)S(1)} %get-tuple-element.243), kind=kLoop, calls=%fused_computation.4.clone.1 | loop fusion | flops 8384512 | bytes 12603392 | tf_op jit(solution)/shard_map/while/body/eval_jaxpr/reduce_sum | solution.py:27
  223.2 4.7 convolution_add_fusion.4
  227.9 0.0 copy-start.3
  228.0 1.3 copy-done.3
  229.3 0.0 all-reduce.3.cloned.1.call-update
  229.3 0.0 all-reduce.5.cloned.1.call-start
  229.4 35.4 %psum.29 = f32[2,2048]{1,0:T(2,128)S(1)} all-reduce(f32[2,2048]{1,0:T(2,128)S(1)} %get-tuple-element.69), channel_id=1, replica_groups=mesh['wide'=8,'narrow'=4] {'wide'}, use_global_device_ids=true, to_apply=%region_7.8 | all-reduce | flops 4096 | bytes 32768 | tf_op jit(solution)/shard_map/psum | solution.py:56
  264.8 65.7 %all-reduce.3.cloned.1.call-done = f32[2,2048,128]{2,1,0:T(8,128)} async-done(((f32[2,2048,128]{2,1,0:T(8,128)}), f32[2,2048,128]{2,1,0:T(8,128)}) %all-reduce.3.cloned.1.call-update) | async-done | bytes 2097168 | tf_op jit(solution)/shard_map/psum | solution.py:56
  330.5 2.9 multiply_reduce_fusion
  333.4 1.3 copy-done.5
  334.7 1.1 convert_element_type.56
  335.8 69.5 %while.27 = (s32[]{:T(128)}, f32[2,2048,128]{2,1,0:T(8,128)S(1)}, f32[2,2048]{1,0:T(2,128)S(1)}, bf16[4,512,2,128]{3,1,2,0:T(8,128)(2,1)S(1)}, bf16[2,2048,128]{...) while((s32[]{:T(128)}, f32[2,2048,128]{2,1,0:T(8,128)S(1)}, ...), condition=%wide.region_13.14_spmd.clone, body=%wide.region_9.0_spmd.clone.sunk | while | flops 1093670912 | bytes 31023212 | solution.py:33
  335.8 7.1 %fusion.92 = (f32[2,512]{1,0:T(2,128)S(1)}, f32[2,512,2048]{2,1,0:T(8,128)}) fusion(f32[2,2048]{1,0:T(2,128)S(1)} %get-tuple-element.301, bf16[2,2048,128]{2,1,0:T(8,128)(2,1)} %get-tuple-element.300, bf16[4,512,2,128]{3,1,2,0:T(8,128)(2,1)S(1)} %get-tuple-element.299, s32[]{:T(128)S(6)} %copy.34), kind=kOutput, calls=%fused_computation.71.clone.1 | convolution fusion | flops 547358720 | bytes 9719812 | tf_op jit(solution)/shard_map/while/body/eval_jaxpr/sub | solution.py:23
  342.9 5.5 %convert_reduce_fusion.5 = (f32[2,2048]{1,0:T(2,128)S(1)}, bf16[2,512,2048]{2,1,0:T(8,128)(2,1)}) fusion(f32[2,512,2048]{2,1,0:T(8,128)} %get-tuple-element.252, f32[2,512]{1,0:T(2,128)S(1)} %get-tuple-element.253), kind=kLoop, calls=%fused_computation.28.clone.1 | loop fusion | flops 8384512 | bytes 12603392 | tf_op jit(solution)/shard_map/while/body/eval_jaxpr/reduce_sum | solution.py:27
  348.4 4.7 convolution_add_fusion.5
  353.2 7.2 %fusion.92 = (f32[2,512]{1,0:T(2,128)S(1)}, f32[2,512,2048]{2,1,0:T(8,128)}) fusion(f32[2,2048]{1,0:T(2,128)S(1)} %get-tuple-element.301, bf16[2,2048,128]{2,1,0:T(8,128)(2,1)} %get-tuple-element.300, bf16[4,512,2,128]{3,1,2,0:T(8,128)(2,1)S(1)} %get-tuple-element.299, s32[]{:T(128)S(6)} %copy.34), kind=kOutput, calls=%fused_computation.71.clone.1 | convolution fusion | flops 547358720 | bytes 9719812 | tf_op jit(solution)/shard_map/while/body/eval_jaxpr/sub | solution.py:23
  360.3 5.5 %convert_reduce_fusion.5 = (f32[2,2048]{1,0:T(2,128)S(1)}, bf16[2,512,2048]{2,1,0:T(8,128)(2,1)}) fusion(f32[2,512,2048]{2,1,0:T(8,128)} %get-tuple-element.252, f32[2,512]{1,0:T(2,128)S(1)} %get-tuple-element.253), kind=kLoop, calls=%fused_computation.28.clone.1 | loop fusion | flops 8384512 | bytes 12603392 | tf_op jit(solution)/shard_map/while/body/eval_jaxpr/reduce_sum | solution.py:27
  365.8 4.7 convolution_add_fusion.5
  370.5 7.2 %fusion.92 = (f32[2,512]{1,0:T(2,128)S(1)}, f32[2,512,2048]{2,1,0:T(8,128)}) fusion(f32[2,2048]{1,0:T(2,128)S(1)} %get-tuple-element.301, bf16[2,2048,128]{2,1,0:T(8,128)(2,1)} %get-tuple-element.300, bf16[4,512,2,128]{3,1,2,0:T(8,128)(2,1)S(1)} %get-tuple-element.299, s32[]{:T(128)S(6)} %copy.34), kind=kOutput, calls=%fused_computation.71.clone.1 | convolution fusion | flops 547358720 | bytes 9719812 | tf_op jit(solution)/shard_map/while/body/eval_jaxpr/sub | solution.py:23
  377.7 5.5 %convert_reduce_fusion.5 = (f32[2,2048]{1,0:T(2,128)S(1)}, bf16[2,512,2048]{2,1,0:T(8,128)(2,1)}) fusion(f32[2,512,2048]{2,1,0:T(8,128)} %get-tuple-element.252, f32[2,512]{1,0:T(2,128)S(1)} %get-tuple-element.253), kind=kLoop, calls=%fused_computation.28.clone.1 | loop fusion | flops 8384512 | bytes 12603392 | tf_op jit(solution)/shard_map/while/body/eval_jaxpr/reduce_sum | solution.py:27
  383.2 4.7 convolution_add_fusion.5
  387.9 7.2 %fusion.92 = (f32[2,512]{1,0:T(2,128)S(1)}, f32[2,512,2048]{2,1,0:T(8,128)}) fusion(f32[2,2048]{1,0:T(2,128)S(1)} %get-tuple-element.301, bf16[2,2048,128]{2,1,0:T(8,128)(2,1)} %get-tuple-element.300, bf16[4,512,2,128]{3,1,2,0:T(8,128)(2,1)S(1)} %get-tuple-element.299, s32[]{:T(128)S(6)} %copy.34), kind=kOutput, calls=%fused_computation.71.clone.1 | convolution fusion | flops 547358720 | bytes 9719812 | tf_op jit(solution)/shard_map/while/body/eval_jaxpr/sub | solution.py:23
  395.1 5.5 %convert_reduce_fusion.5 = (f32[2,2048]{1,0:T(2,128)S(1)}, bf16[2,512,2048]{2,1,0:T(8,128)(2,1)}) fusion(f32[2,512,2048]{2,1,0:T(8,128)} %get-tuple-element.252, f32[2,512]{1,0:T(2,128)S(1)} %get-tuple-element.253), kind=kLoop, calls=%fused_computation.28.clone.1 | loop fusion | flops 8384512 | bytes 12603392 | tf_op jit(solution)/shard_map/while/body/eval_jaxpr/reduce_sum | solution.py:27
  400.6 4.7 convolution_add_fusion.5
  405.3 0.0 copy-start.4
  405.3 1.3 copy-done.4
  406.6 0.0 all-reduce.5.cloned.1.call-update
  406.6 0.0 copy-start.8
  406.6 3.0 copy.15
  409.6 2.7 fusion.54
  412.3 36.7 %psum.31 = f32[2,2048]{1,0:T(2,128)S(1)} all-reduce(f32[2,2048]{1,0:T(2,128)S(1)} %get-tuple-element.71), channel_id=1, replica_groups=mesh['wide'=8,'narrow'=4] {'wide'}, use_global_device_ids=true, to_apply=%region_15.16 | all-reduce | flops 4096 | bytes 32768 | tf_op jit(solution)/shard_map/psum | solution.py:56
  449.0 59.9 %all-reduce.5.cloned.1.call-done = f32[2,2048,128]{2,1,0:T(8,128)} async-done(((f32[2,2048,128]{2,1,0:T(8,128)}), f32[2,2048,128]{2,1,0:T(8,128)}) %all-reduce.5.cloned.1.call-update) | async-done | bytes 2097168 | tf_op jit(solution)/shard_map/psum | solution.py:56
  508.9 2.9 add_divide_fusion
  (30 shorter events, 0.3 us)
Async XLA Ops:
  7.2 7.3 %copy-start = (s32[16384]{0:T(1024)S(1)}, s32[16384]{0:T(1024)}, u32[]{:S(2)}) copy-start(s32[16384]{0:T(1024)} %param.13) | copy-start | bytes 196612
  7.2 130.2 %all-gather.2.cloned.1.call-start = ((), (), s32[]{:S(2)}) async-start(), calls=%async_computation.1 | async-start | bytes 9437184 | tf_op jit(solution)/shard_map/all_gather | solution.py:42
  7.9 6.6 %copy-start.9 = (s32[2048]{0:T(1024)S(1)}, s32[2048]{0:T(1024)}, u32[]{:S(2)}) copy-start(s32[2048]{0:T(1024)} %param.14) | copy-start | bytes 24580
  10.2 31.9 %all-to-all-start = ((bf16[512,4,256]{0,2,1:T(8,128)(2,1)}), bf16[512,4,256]{0,2,1:T(8,128)(2,1)S(1)}, u32[]{:S(2)}, u32[]{:S(2)}) async-start(bf16[512,4,256]{0,2,1:T(8,128)(2,1)} %bitcast), calls=%async_computation | async-start | bytes 2097152 | tf_op jit(solution)/shard_map/all_to_all | solution.py:38
  14.5 316.0 %all-reduce.3.cloned.1.call-start = ((), (), s32[]{:S(2)}) async-start(), calls=%async_computation.2 | async-start | bytes 4194304 | tf_op jit(solution)/shard_map/psum | solution.py:56
  14.5 11.8 %copy-start.2 = (s32[16384]{0:T(1024)S(1)}, s32[16384]{0:T(1024)}, u32[]{:S(2)}) copy-start(s32[16384]{0:T(1024)} %param.12) | copy-start | bytes 196612
  148.5 5.1 copy-start.7
  227.9 1.3 copy-start.3
  229.3 279.6 %all-reduce.5.cloned.1.call-start = ((), (), s32[]{:S(2)}) async-start(), calls=%async_computation.3 | async-start | bytes 4194304 | tf_op jit(solution)/shard_map/psum | solution.py:56
  333.3 1.3 copy-start.5
  405.3 1.3 copy-start.4
  406.6 3.0 copy-start.8
  409.6 99.3 %copy-start.6 = (f32[2,2048,128]{2,1,0:T(8,128)S(1)}, f32[2,2048,128]{2,1,0:T(8,128)}, u32[]{:S(2)}) copy-start(f32[2,2048,128]{2,1,0:T(8,128)} %copy-done.5) | copy-start | bytes 6291460
  449.0 62.8 %copy-start.1 = (s32[16384]{0:T(1024)S(1)}, s32[16384]{0:T(1024)}, u32[]{:S(2)}) copy-start(s32[16384]{0:T(1024)} %param.13) | copy-start | bytes 196612
Sparse Core Ops, SparseCore 0:
  10.1 127.1 all-gather.1
  229.4 101.0 all-reduce.2
  406.7 102.1 all-reduce.4
where the time goes:
time: 519 us; the launch traced here: 518 us
  waiting for transfers between devices  219 us (42%)
  matrix products  94.6 us (18%)
  blocking collectives  72.1 us (14%)
  other arithmetic  63.7 us (12%)
  local copies, waits for them, and re-layouts  50.5 us (10%)
  between operations  14 us (3%)
    psum x2, waiting for transfers between devices, on_device(): totals, counts = lax.psum((totals, counts), 'wide')  126 us
    all_gather x1, waiting for transfers between devices, on_device(): whole = lax.all_gather(centroid_table, 'wide', axis=0, tiled=True)  92.6 us
    psum x2, blocking collectives, on_device(): totals, counts = lax.psum((totals, counts), 'wide')  72.1 us
    sub x8, matrix products, block_step(): weights_soft = jax.nn.softmax(score_matrix, axis=2).astype(jnp.bfloat16)  57.2 us
    reduce_sum x8, other arithmetic, block_step(): jnp.sum(weights_soft, axis=1, dtype=jnp.float32)  44.1 us
    dot_general x8, matrix products, block_step(): jnp.einsum('mbk,bms->mks', weights_soft, row_block, preferred_element_typ...  37.4 us
    gather x3, local copies, waits for them, and re-layouts, on_device(): jnp.take(whole, owner_of * centroid_table.shape[0] + slot_of, axis=0)  16.1 us
    gather x1, local copies, waits for them, and re-layouts, on_device(): slot_of = slot[assign]  11.8 us
  transfers between devices with their start and end apart: 4, of which 3 were waited for; matrix products, arithmetic and copies ran while one was open for 7% of the time, Pallas kernels for 0%

commit v1 on v0

--- a/solution.py
+++ b/solution.py
@@ -6,6 +6,27 @@
 ITERS = 2
 softness_level = 16.0
 prior_weight = 1.0
+
+
+def ring_gather(shard, axis, dim):
+    size, index, extent = (lax.axis_size(axis), lax.axis_index(axis), shard.shape[dim])
+    ahead = [(i, (i + 1) % size) for i in range(size)]
+    left = [(i, (i - 1) % size) for i in range(size)]
+    out = jnp.zeros((*shard.shape[:dim], size * extent, *shard.shape[dim + 1 :]), shard.dtype)
+    out = lax.dynamic_update_slice_in_dim(out, shard, index * extent, axis=dim)
+    from_left = from_right = shard
+    middle = size // 2
+    for step in range(1, middle + 1):
+        from_left = lax.ppermute(from_left, axis, ahead)
+        out = lax.dynamic_update_slice_in_dim(
+            out, from_left, (index - step) % size * extent, axis=dim
+        )
+        if step < size - middle:
+            from_right = lax.ppermute(from_right, axis, left)
+            out = lax.dynamic_update_slice_in_dim(
+                out, from_right, (index + step) % size * extent, axis=dim
+            )
+    return out
 
 
 def score_pass(blocks, narrow_words, codeword_norm_values):
@@ -39,7 +60,7 @@
     group_rows = regrouped.shape[0]
     owner_of = owner[assign]
     slot_of = slot[assign]
-    whole = lax.all_gather(centroid_table, "wide", axis=0, tiled=True)
+    whole = ring_gather(centroid_table, "wide", 0)
     centre = jnp.take(whole, owner_of * centroid_table.shape[0] + slot_of, axis=0)
     residual = (regrouped.astype(jnp.float32) - centre.astype(jnp.float32)).astype(jnp.bfloat16)
     spaces = codebook.shape[0]

time: 519 us -> 558 us (1.075)
  starting transfers between devices: 4.35 us -> 23.3 us
  local copies, waits for them, and re-layouts: 50.5 us -> 68.8 us
    ppermute x0 -> x7, waiting for transfers between devices: none -> 93.8 us  [the longest x4 93.8 us: ring_gather(): from_left = lax.ppermute(from_left, axis, ahead)]
    all_gather x1 -> x0, waiting for transfers between devices: 92.6 us -> none  [on_device(): whole = lax.all_gather(centroid_table, 'wide', axis=0, tiled=True)]
    ppermute x0 -> x7, starting transfers between devices: none -> 19.7 us  [the longest x4 10.5 us: ring_gather(): from_left = lax.ppermute(from_left, axis, ahead)]
    dynamic_update_slice x0 -> x8, local copies, waits for them, and re-layouts: none -> 14.6 us  [the longest x4 7.91 us: ring_gather(): lax.dynamic_update_slice_in_dim(out, from_left, (index - step) % size * e...]
  transfers between devices with their start and end apart: 4 -> 10, of which waited for: 3 -> 6; matrix products, arithmetic and copies ran while one was open for 7% -> 10% of each run, Pallas kernels for 0% -> 0%
where the time goes in v1:
time: 558 us; the launch traced here: 557 us
  waiting for transfers between devices  219 us (39%)
  matrix products  94.6 us (17%)
  blocking collectives  72.5 us (13%)
  local copies, waits for them, and re-layouts  68.8 us (12%)
  other arithmetic  64.6 us (12%)
  starting transfers between devices  23.3 us (4%)
  between operations  14.2 us (3%)
    psum x2, waiting for transfers between devices, on_device(): totals, counts = lax.psum((totals, counts), 'wide')  125 us
    ppermute x4, waiting for transfers between devices, ring_gather(): from_left = lax.ppermute(from_left, axis, ahead)  93.8 us
    psum x2, blocking collectives, on_device(): totals, counts = lax.psum((totals, counts), 'wide')  72.5 us
    sub x8, matrix products, block_step(): weights_soft = jax.nn.softmax(score_matrix, axis=2).astype(jnp.bfloat16)  57.2 us
    reduce_sum x8, other arithmetic, block_step(): jnp.sum(weights_soft, axis=1, dtype=jnp.float32)  44.1 us
    dot_general x8, matrix products, block_step(): jnp.einsum('mbk,bms->mks', weights_soft, row_block, preferred_element_typ...  37.4 us
    gather x3, local copies, waits for them, and re-layouts, on_device(): jnp.take(whole, owner_of * centroid_table.shape[0] + slot_of, axis=0)  16.1 us
    gather x1, local copies, waits for them, and re-layouts, on_device(): slot_of = slot[assign]  11.8 us
  transfers between devices with their start and end apart: 10, of which 6 were waited for; matrix products, arithmetic and copies ran while one was open for 10% of the time, Pallas kernels for 0%

profile of v1, /device:TPU:0, one launch (start us, length us, event | category | flops | bytes accessed | tf_op | source)
XLA Modules:
  0.0 557.2 jit_solution(17498703096979642968)
XLA Ops:
  7.2 3.0 collective-permute-start
  10.2 3.1 collective-permute-start.1
  13.3 2.3 copy.14
  15.6 3.5 all-to-all-start
  19.9 11.8 %gather_fusion = s32[2048]{0:T(1024)S(1)} fusion(s32[16384]{0:T(1024)S(1)} %copy-done, s32[2048]{0:T(1024)S(1)} %fusion.55), kind=kCustom, calls=%fused_computation | custom fusion | bytes 24576 | tf_op jit(solution)/shard_map/gather | solution.py:61
  31.7 11.8 %gather_fusion.1 = s32[2048]{0:T(1024)S(1)} fusion(s32[16384]{0:T(1024)S(1)} %copy-done.2, s32[2048]{0:T(1024)S(1)} %fusion.55), kind=kCustom, calls=%fused_computation.1 | custom fusion | bytes 24576 | tf_op jit(solution)/shard_map/gather | solution.py:62
  43.5 11.9 %collective-permute-done = bf16[2048,256]{1,0:T(8,128)(2,1)} collective-permute-done((bf16[2048,256]{1,0:T(8,128)(2,1)}, bf16[2048,256]{1,0:T(8,128)(2,1)}, u32[]{:S(2)}, u32[]{:S(2)}) %collective-permute-start) | collective-permute-done | bytes 1048608 | tf_op jit(solution)/shard_map/ppermute | solution.py:20
  55.4 2.5 collective-permute-start.2
  57.9 3.6 broadcast_in_dim.31
  62.6 3.1 collective-permute-start.3
  65.7 36.6 %collective-permute-done.2 = bf16[2048,256]{1,0:T(8,128)(2,1)} collective-permute-done((bf16[2048,256]{1,0:T(8,128)(2,1)}, bf16[2048,256]{1,0:T(8,128)(2,1)}, u32[]{:S(2)}, u32[]{:S(2)}) %collective-permute-start.2) | collective-permute-done | bytes 1048608 | tf_op jit(solution)/shard_map/ppermute | solution.py:20
  102.2 2.5 collective-permute-start.4
  104.7 3.9 multiply_reduce_fusion.1
  108.6 2.6 fusion.66
  111.2 3.0 collective-permute-start.5
  114.3 2.3 constant_dynamic-update-slice_fusion.6
  116.6 31.7 %collective-permute-done.4 = bf16[2048,256]{1,0:T(8,128)(2,1)} collective-permute-done((bf16[2048,256]{1,0:T(8,128)(2,1)}, bf16[2048,256]{1,0:T(8,128)(2,1)}, u32[]{:S(2)}, u32[]{:S(2)}) %collective-permute-start.4) | collective-permute-done | bytes 1048608 | tf_op jit(solution)/shard_map/ppermute | solution.py:20
  148.2 2.5 collective-permute-start.6
  150.7 2.3 constant_dynamic-update-slice_fusion.5
  153.0 2.3 constant_dynamic-update-slice_fusion.4
  155.3 2.3 constant_dynamic-update-slice_fusion.3
  157.6 2.3 constant_dynamic-update-slice_fusion.2
  161.0 13.6 %collective-permute-done.6 = bf16[2048,256]{1,0:T(8,128)(2,1)S(1)} collective-permute-done((bf16[2048,256]{1,0:T(8,128)(2,1)}, bf16[2048,256]{1,0:T(8,128)(2,1)S(1)}, u32[]{:S(2)}, u32[]{:S(2)}) %collective-permute-start.6) | collective-permute-done | bytes 1048608 | tf_op jit(solution)/shard_map/ppermute | solution.py:20
  175.6 11.1 %gather_fusion.2 = bf16[2048,256]{1,0:T(8,128)(2,1)S(1)} fusion(bf16[16384,256]{1,0:T(8,128)(2,1)} %constant_dynamic-update-slice_fusion, s32[2048]{0:T(1024)S(1)} %broadcast_clamp_fusion), kind=kCustom, calls=%fused_computation.2 | custom fusion | bytes 2105344 | tf_op jit(solution)/shard_map/jit(_take)/gather | solution.py:64
  186.7 1.4 gather.15
  188.1 3.7 copy.16
  191.7 3.3 subtract_convert_fusion
  195.0 1.6 copy.18
  196.6 69.5 %while.26 = (s32[]{:T(128)}, f32[2,2048,128]{2,1,0:T(8,128)S(1)}, f32[2,2048]{1,0:T(2,128)S(1)}, bf16[4,512,2,128]{3,1,2,0:T(8,128)(2,1)S(1)}, bf16[2,2048,128]{...) while((s32[]{:T(128)}, f32[2,2048,128]{2,1,0:T(8,128)S(1)}, ...), condition=%wide.region_5.6_spmd.clone, body=%wide.region_1.5_spmd.clone.sunk | while | flops 1093670912 | bytes 31023204 | solution.py:54
  196.7 7.2 %fusion.87 = (f32[2,512]{1,0:T(2,128)S(1)}, f32[2,512,2048]{2,1,0:T(8,128)}) fusion(f32[2,2048]{1,0:T(2,128)S(1)} %get-tuple-element.277, bf16[2,2048,128]{2,1,0:T(8,128)(2,1)} %get-tuple-element.276, bf16[4,512,2,128]{3,1,2,0:T(8,128)(2,1)S(1)} %get-tuple-element.275, s32[]{:T(128)} %get-tuple-element.264), kind=kOutput, calls=%fused_computation.78.clone.1 | convolution fusion | flops 547358720 | bytes 9719812 | tf_op jit(solution)/shard_map/while/body/eval_jaxpr/sub | solution.py:44
  203.8 5.5 convert_reduce_fusion.4
  209.3 4.7 convolution_add_fusion.4
  214.0 7.2 %fusion.87 = (f32[2,512]{1,0:T(2,128)S(1)}, f32[2,512,2048]{2,1,0:T(8,128)}) fusion(f32[2,2048]{1,0:T(2,128)S(1)} %get-tuple-element.277, bf16[2,2048,128]{2,1,0:T(8,128)(2,1)} %get-tuple-element.276, bf16[4,512,2,128]{3,1,2,0:T(8,128)(2,1)S(1)} %get-tuple-element.275, s32[]{:T(128)} %get-tuple-element.264), kind=kOutput, calls=%fused_computation.78.clone.1 | convolution fusion | flops 547358720 | bytes 9719812 | tf_op jit(solution)/shard_map/while/body/eval_jaxpr/sub | solution.py:44
  221.2 5.5 convert_reduce_fusion.4
  226.7 4.7 convolution_add_fusion.4
  231.4 7.2 %fusion.87 = (f32[2,512]{1,0:T(2,128)S(1)}, f32[2,512,2048]{2,1,0:T(8,128)}) fusion(f32[2,2048]{1,0:T(2,128)S(1)} %get-tuple-element.277, bf16[2,2048,128]{2,1,0:T(8,128)(2,1)} %get-tuple-element.276, bf16[4,512,2,128]{3,1,2,0:T(8,128)(2,1)S(1)} %get-tuple-element.275, s32[]{:T(128)} %get-tuple-element.264), kind=kOutput, calls=%fused_computation.78.clone.1 | convolution fusion | flops 547358720 | bytes 9719812 | tf_op jit(solution)/shard_map/while/body/eval_jaxpr/sub | solution.py:44
  238.6 5.5 convert_reduce_fusion.4
  244.1 4.7 convolution_add_fusion.4
  248.8 7.2 %fusion.87 = (f32[2,512]{1,0:T(2,128)S(1)}, f32[2,512,2048]{2,1,0:T(8,128)}) fusion(f32[2,2048]{1,0:T(2,128)S(1)} %get-tuple-element.277, bf16[2,2048,128]{2,1,0:T(8,128)(2,1)} %get-tuple-element.276, bf16[4,512,2,128]{3,1,2,0:T(8,128)(2,1)S(1)} %get-tuple-element.275, s32[]{:T(128)} %get-tuple-element.264), kind=kOutput, calls=%fused_computation.78.clone.1 | convolution fusion | flops 547358720 | bytes 9719812 | tf_op jit(solution)/shard_map/while/body/eval_jaxpr/sub | solution.py:44
  256.0 5.5 convert_reduce_fusion.4
  261.5 4.7 convolution_add_fusion.4
  266.2 1.3 copy-done.3
  267.6 36.0 %psum.29 = f32[2,2048]{1,0:T(2,128)S(1)} all-reduce(f32[2,2048]{1,0:T(2,128)S(1)} %get-tuple-element.69), channel_id=1, replica_groups=mesh['wide'=8,'narrow'=4] {'wide'}, use_global_device_ids=true, to_apply=%region_7.8 | all-reduce | flops 4096 | bytes 32768 | tf_op jit(solution)/shard_map/psum | solution.py:77
  303.6 65.3 %all-reduce.3.cloned.1.call-done = f32[2,2048,128]{2,1,0:T(8,128)} async-done(((f32[2,2048,128]{2,1,0:T(8,128)}), f32[2,2048,128]{2,1,0:T(8,128)}) %all-reduce.3.cloned.1.call-update) | async-done | bytes 2097168 | tf_op jit(solution)/shard_map/psum | solution.py:77
  368.9 2.9 multiply_reduce_fusion
  371.8 1.3 copy-done.5
  374.3 69.5 %while.27 = (s32[]{:T(128)}, f32[2,2048,128]{2,1,0:T(8,128)S(1)}, f32[2,2048]{1,0:T(2,128)S(1)}, bf16[4,512,2,128]{3,1,2,0:T(8,128)(2,1)S(1)}, bf16[2,2048,128]{...) while((s32[]{:T(128)}, f32[2,2048,128]{2,1,0:T(8,128)S(1)}, ...), condition=%wide.region_13.14_spmd.clone, body=%wide.region_9.13_spmd.clone.sunk | while | flops 1093670912 | bytes 31023204 | solution.py:54
  374.3 7.1 %fusion.92 = (f32[2,512]{1,0:T(2,128)S(1)}, f32[2,512,2048]{2,1,0:T(8,128)}) fusion(f32[2,2048]{1,0:T(2,128)S(1)} %get-tuple-element.301, bf16[2,2048,128]{2,1,0:T(8,128)(2,1)} %get-tuple-element.300, bf16[4,512,2,128]{3,1,2,0:T(8,128)(2,1)S(1)} %get-tuple-element.299, s32[]{:T(128)} %get-tuple-element.288), kind=kOutput, calls=%fused_computation.79.clone.1 | convolution fusion | flops 547358720 | bytes 9719812 | tf_op jit(solution)/shard_map/while/body/eval_jaxpr/sub | solution.py:44
  381.4 5.5 convert_reduce_fusion.5
  386.9 4.7 convolution_add_fusion.5
  391.6 7.2 %fusion.92 = (f32[2,512]{1,0:T(2,128)S(1)}, f32[2,512,2048]{2,1,0:T(8,128)}) fusion(f32[2,2048]{1,0:T(2,128)S(1)} %get-tuple-element.301, bf16[2,2048,128]{2,1,0:T(8,128)(2,1)} %get-tuple-element.300, bf16[4,512,2,128]{3,1,2,0:T(8,128)(2,1)S(1)} %get-tuple-element.299, s32[]{:T(128)} %get-tuple-element.288), kind=kOutput, calls=%fused_computation.79.clone.1 | convolution fusion | flops 547358720 | bytes 9719812 | tf_op jit(solution)/shard_map/while/body/eval_jaxpr/sub | solution.py:44
  398.8 5.5 convert_reduce_fusion.5
  404.3 4.7 convolution_add_fusion.5
  409.0 7.2 %fusion.92 = (f32[2,512]{1,0:T(2,128)S(1)}, f32[2,512,2048]{2,1,0:T(8,128)}) fusion(f32[2,2048]{1,0:T(2,128)S(1)} %get-tuple-element.301, bf16[2,2048,128]{2,1,0:T(8,128)(2,1)} %get-tuple-element.300, bf16[4,512,2,128]{3,1,2,0:T(8,128)(2,1)S(1)} %get-tuple-element.299, s32[]{:T(128)} %get-tuple-element.288), kind=kOutput, calls=%fused_computation.79.clone.1 | convolution fusion | flops 547358720 | bytes 9719812 | tf_op jit(solution)/shard_map/while/body/eval_jaxpr/sub | solution.py:44
  416.2 5.5 convert_reduce_fusion.5
  421.7 4.7 convolution_add_fusion.5
  426.4 7.2 %fusion.92 = (f32[2,512]{1,0:T(2,128)S(1)}, f32[2,512,2048]{2,1,0:T(8,128)}) fusion(f32[2,2048]{1,0:T(2,128)S(1)} %get-tuple-element.301, bf16[2,2048,128]{2,1,0:T(8,128)(2,1)} %get-tuple-element.300, bf16[4,512,2,128]{3,1,2,0:T(8,128)(2,1)S(1)} %get-tuple-element.299, s32[]{:T(128)} %get-tuple-element.288), kind=kOutput, calls=%fused_computation.79.clone.1 | convolution fusion | flops 547358720 | bytes 9719812 | tf_op jit(solution)/shard_map/while/body/eval_jaxpr/sub | solution.py:44
  433.5 5.5 convert_reduce_fusion.5
  439.1 4.7 convolution_add_fusion.5
  445.1 3.0 copy.15
  448.1 2.9 fusion.54
  451.1 36.5 %psum.31 = f32[2,2048]{1,0:T(2,128)S(1)} all-reduce(f32[2,2048]{1,0:T(2,128)S(1)} %get-tuple-element.71), channel_id=1, replica_groups=mesh['wide'=8,'narrow'=4] {'wide'}, use_global_device_ids=true, to_apply=%region_15.16 | all-reduce | flops 4096 | bytes 32768 | tf_op jit(solution)/shard_map/psum | solution.py:77
  487.5 59.9 %all-reduce.5.cloned.1.call-done = f32[2,2048,128]{2,1,0:T(8,128)} async-done(((f32[2,2048,128]{2,1,0:T(8,128)}), f32[2,2048,128]{2,1,0:T(8,128)}) %all-reduce.5.cloned.1.call-update) | async-done | bytes 2097168 | tf_op jit(solution)/shard_map/psum | solution.py:77
  547.4 2.9 add_divide_fusion
  (48 shorter events, 6.6 us)
Async XLA Ops:
  7.2 12.7 %copy-start = (s32[16384]{0:T(1024)S(1)}, s32[16384]{0:T(1024)}, u32[]{:S(2)}) copy-start(s32[16384]{0:T(1024)} %param.12) | copy-start | bytes 196612
  7.2 24.5 %copy-start.2 = (s32[16384]{0:T(1024)S(1)}, s32[16384]{0:T(1024)}, u32[]{:S(2)}) copy-start(s32[16384]{0:T(1024)} %param.13) | copy-start | bytes 196612
  7.2 48.2 %collective-permute-start = (bf16[2048,256]{1,0:T(8,128)(2,1)}, bf16[2048,256]{1,0:T(8,128)(2,1)}, u32[]{:S(2)}, u32[]{:S(2)}) collective-permute-start(bf16[2048,256]{1,0:T(8,128)(2,1)} %param.11), channel_id=1, source_target_pairs={{0,4},{4,8},{8,12},{12,16},{16,20},{20,24},{24,28},{28,0},{1,5},{5... | collective-permute-start | bytes 3145736 | tf_op jit(solution)/shard_map/ppermute | solution.py:20
  10.2 52.4 %collective-permute-start.1 = (bf16[2048,256]{1,0:T(8,128)(2,1)}, bf16[2048,256]{1,0:T(8,128)(2,1)}, u32[]{:S(2)}, u32[]{:S(2)}) collective-permute-start(bf16[2048,256]{1,0:T(8,128)(2,1)} %param.11), channel_id=1, source_target_pairs={{0,28},{4,0},{8,4},{12,8},{16,12},{20,16},{24,20},{28,24},{1,29},{... | collective-permute-start | bytes 3145736 | tf_op jit(solution)/shard_map/ppermute | solution.py:25
  15.6 93.0 %all-to-all-start = ((bf16[512,4,256]{0,2,1:T(8,128)(2,1)}), bf16[512,4,256]{0,2,1:T(8,128)(2,1)S(1)}, u32[]{:S(2)}, u32[]{:S(2)}) async-start(bf16[512,4,256]{0,2,1:T(8,128)(2,1)} %bitcast), calls=%async_computation | async-start | bytes 2097152 | tf_op jit(solution)/shard_map/all_to_all | solution.py:59
  19.1 349.8 %all-reduce.3.cloned.1.call-start = ((), (), s32[]{:S(2)}) async-start(), calls=%async_computation.1 | async-start | bytes 4194304 | tf_op jit(solution)/shard_map/psum | solution.py:77
  31.7 29.8 %copy-start.8 = (bf16[2048,256]{1,0:T(8,128)(2,1)S(1)}, bf16[2048,256]{1,0:T(8,128)(2,1)}, u32[]{:S(2)}) copy-start(bf16[2048,256]{1,0:T(8,128)(2,1)} %param.11) | copy-start | bytes 3145732
  55.4 46.8 %collective-permute-start.2 = (bf16[2048,256]{1,0:T(8,128)(2,1)}, bf16[2048,256]{1,0:T(8,128)(2,1)}, u32[]{:S(2)}, u32[]{:S(2)}) collective-permute-start(bf16[2048,256]{1,0:T(8,128)(2,1)} %collective-permute-done), channel_id=1, source_target_pairs={{0,4},{4,8},{8,12},{12,16},{16,20},{20,24},{24,28},{28,0},{1,5},{5... | collective-permute-start | bytes 3145736 | tf_op jit(solution)/shard_map/ppermute | solution.py:20
  62.6 48.7 %collective-permute-start.3 = (bf16[2048,256]{1,0:T(8,128)(2,1)}, bf16[2048,256]{1,0:T(8,128)(2,1)}, u32[]{:S(2)}, u32[]{:S(2)}) collective-permute-start(bf16[2048,256]{1,0:T(8,128)(2,1)} %collective-permute-done.1), channel_id=1, source_target_pairs={{0,28},{4,0},{8,4},{12,8},{16,12},{20,16},{24,20},{28,24},{1,29},{... | collective-permute-start | bytes 3145736 | tf_op jit(solution)/shard_map/ppermute | solution.py:25
  102.2 46.0 %collective-permute-start.4 = (bf16[2048,256]{1,0:T(8,128)(2,1)}, bf16[2048,256]{1,0:T(8,128)(2,1)}, u32[]{:S(2)}, u32[]{:S(2)}) collective-permute-start(bf16[2048,256]{1,0:T(8,128)(2,1)} %collective-permute-done.2), channel_id=1, source_target_pairs={{0,4},{4,8},{8,12},{12,16},{16,20},{20,24},{24,28},{28,0},{1,5},{5... | collective-permute-start | bytes 3145736 | tf_op jit(solution)/shard_map/ppermute | solution.py:20
  111.2 48.7 %collective-permute-start.5 = (bf16[2048,256]{1,0:T(8,128)(2,1)}, bf16[2048,256]{1,0:T(8,128)(2,1)S(1)}, u32[]{:S(2)}, u32[]{:S(2)}) collective-permute-start(bf16[2048,256]{1,0:T(8,128)(2,1)} %collective-permute-done.3), channel_id=1, source_target_pairs={{0,28},{4,0},{8,4},{12,8},{16,12},{20,16},{24,20},{28,24},{1,29},{... | collective-permute-start | bytes 3145736 | tf_op jit(solution)/shard_map/ppermute | solution.py:25
  148.2 26.3 %collective-permute-start.6 = (bf16[2048,256]{1,0:T(8,128)(2,1)}, bf16[2048,256]{1,0:T(8,128)(2,1)S(1)}, u32[]{:S(2)}, u32[]{:S(2)}) collective-permute-start(bf16[2048,256]{1,0:T(8,128)(2,1)} %collective-permute-done.4), channel_id=1, source_target_pairs={{0,4},{4,8},{8,12},{12,16},{16,20},{20,24},{24,28},{28,0},{1,5},{5... | collective-permute-start | bytes 3145736 | tf_op jit(solution)/shard_map/ppermute | solution.py:20
  186.7 5.1 copy-start.7
  266.2 1.3 copy-start.3
  267.5 279.9 %all-reduce.5.cloned.1.call-start = ((), (), s32[]{:S(2)}) async-start(), calls=%async_computation.2 | async-start | bytes 4194304 | tf_op jit(solution)/shard_map/psum | solution.py:77
  371.8 1.3 copy-start.5
  443.8 1.3 copy-start.4
  443.8 106.5 %copy-start.1 = (s32[16384]{0:T(1024)S(1)}, s32[16384]{0:T(1024)}, u32[]{:S(2)}) copy-start(s32[16384]{0:T(1024)} %param.12) | copy-start | bytes 196612
  445.1 102.3 %copy-start.6 = (f32[2,2048,128]{2,1,0:T(8,128)S(1)}, f32[2,2048,128]{2,1,0:T(8,128)}, u32[]{:S(2)}) copy-start(f32[2,2048,128]{2,1,0:T(8,128)} %copy-done.5) | copy-start | bytes 6291460
Sparse Core Ops, SparseCore 0:
  267.6 101.2 all-reduce.2
  445.2 102.1 all-reduce.4
